TPU v7x, 32 devices: a whole 2x2x4 slice. The times are simulated.
32 devices in a mesh: groups: 2 (over x), lon: 16 (over z, y, core).
Axes of the slice: x: 2, y: 2, z: 4, core: 2. Of those that a mesh axis runs over, the one named last changes fastest.
Arguments:
- fields: bfloat16 [128, 512, 256], P('groups', 'lon'), parts along dimension 0, may hold values from -36 to 36
- sea_mask: int32 [128, 512], P('groups', 'lon'), parts along dimension 0, may hold values 0 or 1
- cotangent: bfloat16 [128, 512, 256], P('groups', 'lon'), parts along dimension 0, may hold values from -6 to 6
- depth_kernel: float32 [7, 7, 256], replicated, may hold values from -0.875 to 0.875
- norm_gain: float32 [256], replicated, may hold values from 0.1 to 1.9
- up_weight: bfloat16 [256, 1024], replicated, may hold values from -0.375 to 0.375
- down_weight: bfloat16 [256, 1024], replicated, may hold values from -0.1875 to 0.1875
- layer_scale: float32 [256], replicated, may hold values from 0.3 to 3
Outputs:
- grad_fields: bfloat16 [128, 512, 256], P('groups', 'lon'), parts along dimension 0
- grad_kernel: float32 [14, 7, 256], P('groups'), parts along dimension 0
- grad_up: float32 [256, 2048], P('lon', 'groups'), parts along dimension 1
- grad_down: float32 [256, 2048], P('lon', 'groups'), parts along dimension 1
There are 2 independent parts, one for each index of `groups`. A program takes and returns all parts, laid end to end along the dimension named above; an argument that names none is the same for every part. Nothing has to cross between parts.
All inputs are finite; a program needn't handle non-finite values. No bound on the sum of `sea_mask` on one device may be relied on, other than what follows from the above.
Results may differ from a plain program's by a relative error of at most 0.0063.
Values may be sent and summed in bfloat16 or wider, within the bound.
A program may use at most 128 MiB of HBM per device.

v0:
```python
import math

import jax
import jax.numpy as jnp
from jax import lax
from jax.sharding import PartitionSpec as P


def from_partner(block, axis, bit):
    count = lax.axis_size(axis)
    route = []
    for low in range(count):
        high = low | 1 << bit
        if high != low and high < count:
            route += [(low, high), (high, low)]
    return lax.ppermute(block, axis, route)


def extended_2(cells, sides, width):
    for axis, dim in sides:
        count = lax.axis_size(axis)
        head = lax.slice_in_dim(cells, 0, width, axis=dim)
        tail = lax.slice_in_dim(cells, cells.shape[dim] - width, cells.shape[dim], axis=dim)
        cells = jnp.concatenate(
            [
                lax.ppermute(tail, axis, [(i, (i + 1) % count) for i in range(count)]),
                cells,
                lax.ppermute(head, axis, [((i + 1) % count, i) for i in range(count)]),
            ],
            axis=dim,
        )
    return cells


def gelu_tanh(values):
    return jax.nn.gelu(values, approximate=True)


def local(
    fields, sea_mask, cotangent, depth_kernel, norm_gain, up_weight, down_weight, layer_scale
):
    band_rows, band_cols, channels = fields.shape
    devices = lax.axis_size("lon")
    mask_bf = sea_mask.astype(jnp.bfloat16)[:, :, None]
    masked = fields * mask_bf
    seam_rows = masked[band_rows - 3 :]
    partner_rows = seam_rows
    for bit in range(devices.bit_length() - 1):
        partner_rows = from_partner(partner_rows, "lon", bit)
    ghost = partner_rows[::-1, ::-1]
    south = jnp.zeros((3, band_cols, channels), jnp.bfloat16)
    padded = jnp.concatenate([south, masked, ghost], axis=0)
    extended = extended_2(padded, (("lon", 1),), 3)
    ext_wide = extended.astype(jnp.float32)
    conv = jnp.zeros((band_rows, band_cols, channels), jnp.float32)
    for row_tap in range(7):
        for col_tap in range(7):
            conv = (
                conv
                + depth_kernel[row_tap, col_tap]
                * ext_wide[row_tap : row_tap + band_rows, col_tap : col_tap + band_cols]
            )
    mean_z = jnp.mean(conv, axis=-1, keepdims=True)
    centred = conv - mean_z
    inv_std = lax.rsqrt(jnp.mean(centred * centred, axis=-1, keepdims=True) + 1e-06)
    nhat = centred * inv_std
    cells = band_rows * band_cols
    normed = (nhat * norm_gain).astype(jnp.bfloat16).reshape(cells, channels)
    dout = (
        (cotangent.astype(jnp.float32) * layer_scale * mask_bf.astype(jnp.float32))
        .astype(jnp.bfloat16)
        .reshape(cells, channels)
    )
    preact = jnp.dot(normed, up_weight, preferred_element_type=jnp.float32)
    hidden = gelu_tanh(preact).astype(jnp.bfloat16)
    dhid = jnp.dot(dout, down_weight, preferred_element_type=jnp.float32)
    _, back = jax.vjp(gelu_tanh, preact)
    dpre = back(dhid)[0].astype(jnp.bfloat16)
    contract_rows = (((0,), (0,)), ((), ()))
    contract_cols = (((1,), (1,)), ((), ()))
    factor = 1.0 / math.sqrt(cells * devices)
    hidden_width = up_weight.shape[1]
    term_up = lax.dot_general(normed, dpre, contract_rows, preferred_element_type=jnp.float32)
    term_down = lax.dot_general(dout, hidden, contract_rows, preferred_element_type=jnp.float32)
    owned = lax.psum_scatter(
        jnp.concatenate([term_up, term_down], axis=1) * factor,
        "lon",
        scatter_dimension=0,
        tiled=True,
    )
    grad_up = owned[:, :hidden_width]
    grad_down = owned[:, hidden_width:]
    dnorm = lax.dot_general(dpre, up_weight, contract_cols, preferred_element_type=jnp.float32)
    scaled = dnorm.reshape(band_rows, band_cols, channels) * norm_gain
    grad_conv = inv_std * (
        scaled
        - jnp.mean(scaled, axis=-1, keepdims=True)
        - nhat * jnp.mean(scaled * nhat, axis=-1, keepdims=True)
    )
    taps = []
    for row_tap in range(7):
        for col_tap in range(7):
            taps.append(
                jnp.sum(
                    grad_conv
                    * ext_wide[row_tap : row_tap + band_rows, col_tap : col_tap + band_cols],
                    axis=(0, 1),
                )
            )
    local_kernel = jnp.stack(taps, axis=0).reshape(7, 7, channels) * factor
    grad_kernel = lax.psum(local_kernel, "lon")
    grad_pad = jnp.pad(grad_conv, ((6, 6), (6, 6), (0, 0)))
    grad_ext = jnp.zeros((band_rows + 6, band_cols + 6, channels), jnp.float32)
    for row_tap in range(7):
        for col_tap in range(7):
            grad_ext = (
                grad_ext
                + depth_kernel[row_tap, col_tap]
                * grad_pad[
                    6 - row_tap : 12 - row_tap + band_rows, 6 - col_tap : 12 - col_tap + band_cols
                ]
            )
    rims = jnp.concatenate([grad_ext[:, :3], grad_ext[:, band_cols + 3 :]], axis=1)
    arrived = extended_2(rims.astype(jnp.bfloat16), (("lon", 1),), 3).astype(rims.dtype)
    grad_padded = grad_ext[:, 3 : band_cols + 3]
    grad_padded = grad_padded.at[:, :3].add(arrived[:, :3])
    grad_padded = grad_padded.at[:, band_cols - 3 :].add(arrived[:, 9:])
    seam_grads = grad_padded[band_rows + 3 :]
    partner_grads = seam_grads
    for bit in range(devices.bit_length() - 1):
        partner_grads = from_partner(partner_grads.astype(jnp.bfloat16), "lon", bit).astype(
            partner_grads.dtype
        )
    grad_masked = grad_padded[3 : band_rows + 3]
    grad_masked = grad_masked.at[band_rows - 3 :].add(partner_grads[::-1, ::-1])
    grad_fields = (
        cotangent.astype(jnp.float32) + mask_bf.astype(jnp.float32) * grad_masked
    ).astype(jnp.bfloat16)
    return (grad_fields, grad_kernel, grad_up, grad_down)


def solution(mesh):
    return jax.shard_map(
        local,
        mesh=mesh,
        in_specs=(
            P("groups", "lon", None),
            P("groups", "lon"),
            P("groups", "lon", None),
            P(),
            P(),
            P(),
            P(),
            P(),
        ),
        out_specs=(
            P("groups", "lon", None),
            P("groups", None, None),
            P("lon", "groups"),
            P("lon", "groups"),
        ),
        check_vma=False,
    )
```

profile of v0, /device:TPU:0, one launch (start us, length us, event | category | flops | bytes accessed | tf_op | source)
XLA Modules:
  0.0 221.3 jit_solution(10699872550884711838)
XLA Ops:
  7.2 0.8 convert_element_type.47
  8.2 1.6 broadcast_multiply_fusion
  9.8 0.5 collective-permute-start
  10.4 0.8 collective-permute-done
  11.2 2.9 %collective-permute-start.1 = (bf16[3,32,256]{2,1,0:T(8,128)(2,1)S(1)}, bf16[3,32,256]{2,1,0:T(8,128)(2,1)S(1)}, u32[]{:S(2)}, u32[]{:S(2)}) collective-permute-start(bf16[3,32,256]{2,1,0:T(8,128)(2,1)S(1)} %collective-permute-done), channel_id=1, source_target_pairs={{0,2},{2,0},{1,3},{3,1},{4,6},{6,4},{5,7},{7,5},{8,10},{10,8},{9,1... | collective-permute-start | bytes 147464 | tf_op jit(solution)/shard_map/ppermute | solution.py:16
  14.0 1.3 fusion.106
  15.4 0.7 collective-permute-done.1
  16.1 2.1 collective-permute-start.2
  18.3 2.0 collective-permute-done.2
  20.3 3.0 %collective-permute-start.3 = (bf16[3,32,256]{2,1,0:T(8,128)(2,1)S(1)}, bf16[3,32,256]{2,1,0:T(8,128)(2,1)S(1)}, u32[]{:S(2)}, u32[]{:S(2)}) collective-permute-start(bf16[3,32,256]{2,1,0:T(8,128)(2,1)S(1)} %collective-permute-done.2), channel_id=1, source_target_pairs={{0,8},{8,0},{1,9},{9,1},{2,10},{10,2},{3,11},{11,3},{4,12},{12,4},... | collective-permute-start | bytes 147464 | tf_op jit(solution)/shard_map/ppermute | solution.py:16
  23.3 0.6 fusion.119
  24.0 1.4 collective-permute-done.3
  25.6 4.4 %collective-permute-start.5 = (bf16[70,3,256]{2,1,0:T(4,128)(2,1)S(1)}, bf16[70,3,256]{2,1,0:T(4,128)(2,1)S(1)}, u32[]{:S(2)}, u32[]{:S(2)}) collective-permute-start(bf16[70,3,256]{2,1,0:T(4,128)(2,1)S(1)} %get-tuple-element.97), channel_id=1, source_target_pairs={{1,0},{2,1},{3,2},{4,3},{5,4},{6,5},{7,6},{8,7},{9,8},{10,9},{11,1... | collective-permute-start | bytes 322568 | tf_op jit(solution)/shard_map/ppermute | solution.py:28
  30.3 2.7 %collective-permute-done.4 = bf16[70,3,256]{2,1,0:T(4,128)(2,1)S(1)} collective-permute-done((bf16[70,3,256]{2,1,0:T(4,128)(2,1)S(1)}, bf16[70,3,256]{2,1,0:T(4,128)(2,1)S(1)}, u32[]{:S(2)}, u32[]{:S(2)}) %collective-permute-start.4) | collective-permute-done | bytes 107552 | tf_op jit(solution)/shard_map/ppermute | solution.py:26
  33.0 1.9 maximum_convert_fusion
  35.2 15.9 %fusion.115 = (f32[64,32]{1,0:T(8,128)S(1)}, f32[64,32,256]{2,1,0:T(8,128)}) fusion(f32[70,38,256]{2,1,0:T(8,128)S(1)} %maximum_convert_fusion, f32[256]{0:T(256)S(1)} %bitcast.211, f32[256]{0:T(256)S(1)} %bitcast.213, f32[256]{0:T(256)S(1)} %bitcast.119, f32[256]{0:T(256)S(1)} %bitcast.121, f32[256]{0:T(256)S(1)} %bitcast.123, f32[256]{0:T(256)S(1)} %bitcast.125, ...), kind=kLoop, calls=%fused_computation.242 | loop fusion | flops 51378176 | bytes 104915968 | tf_op jit(solution)/shard_map/reduce_sum | solution.py:63
  51.1 2.4 %multiply_reduce_fusion.51 = f32[64,32]{1,0:T(8,128)S(1)} fusion(f32[64,32,256]{2,1,0:T(8,128)} %get-tuple-element.93, f32[64,32]{1,0:T(8,128)S(1)} %broadcast_multiply_fusion.3), kind=kLoop, calls=%fused_computation.216 | loop fusion | flops 1570816 | bytes 2113536 | tf_op jit(solution)/shard_map/reduce_sum | solution.py:65
  53.5 0.7 multiply_convert_fusion.2
  54.3 1.3 fusion.121
  55.6 0.3 copy-done.11
  55.9 4.2 %fusion.7 = f32[256,1024]{1,0:T(8,128)} fusion(bf16[2048,256]{1,0:T(8,128)(2,1)S(1)} %bitcast.115, f32[2048,1024]{1,0:T(8,128)S(1)} %fusion.121), kind=kOutput, calls=%fused_computation.59 | convolution fusion | flops 1092616192 | bytes 10485760 | tf_op jit(solution)/shard_map/dot_general | solution.py:84
  60.1 6.3 %fusion.6 = bf16[2048,1024]{1,0:T(8,128)(2,1)S(1)} fusion(f32[2048,1024]{1,0:T(8,128)S(1)} %fusion.121, bf16[2048,256]{1,0:T(8,128)(2,1)S(1)} %bitcast.116, bf16[256,1024]{1,0:T(8,128)(2,1)S(1)} %copy-done.109), kind=kOutput, calls=%fused_computation.57 | convolution fusion | flops 1115684864 | bytes 14155776 | tf_op jit(solution)/shard_map/dot_general | solution.py:76
  66.3 2.6 %multiply_reduce_fusion.50 = (f32[2048]{0:T(1024)S(1)}, f32[2048,256]{1,0:T(8,128)}) fusion(f32[256]{0:T(256)S(1)} %copy-done.17, bf16[2048,1024]{1,0:T(8,128)(2,1)S(1)} %fusion.6, bf16[256,1024]{1,0:T(8,128)(2,1)S(1)} %copy-done), kind=kOutput, calls=%fused_computation.214 | convolution fusion | flops 1074788352 | bytes 6824960 | tf_op jit(solution)/shard_map/dot_general | solution.py:93
  69.1 2.9 %multiply_reduce_fusion.49 = f32[64,32]{1,0:T(8,128)S(1)} fusion(f32[64,32,256]{2,1,0:T(8,128)} %bitcast.112, f32[64,32,256]{2,1,0:T(8,128)} %get-tuple-element.93, f32[256]{0:T(256)S(1)} %copy-done.17, f32[64,32]{1,0:T(8,128)S(1)} %add_rsqrt_fusion, f32[64,32]{1,0:T(8,128)S(1)} %broadcast_multiply_fusion.3), kind=kLoop, calls=%fused_computation.213 | loop fusion | flops 2619392 | bytes 4219904 | tf_op jit(solution)/shard_map/reduce_sum | solution.py:98
  72.0 0.5 copy-done.6
  72.9 6.6 %multiply_reduce_fusion = (f32[256]{0:T(256)}, f32[256]{0:T(256)}, f32[256]{0:T(256)}, f32[256]{0:T(256)}, f32[256]{0:T(256)}, /*index=5*/f32[256]{0:T(256)}, f3...) fusion(f32[70,38,256]{2,1,0:T(8,128)S(1)} %maximum_convert_fusi, ...), kind=kLoop, calls=%fused_computation.163 | loop fusion | flops 22539776 | bytes 44092416 | tf_op jit(solution)/shard_map/reduce_sum | solution.py:104
  79.9 22.2 %fusion.113 = (bf16[70,38,256]{2,1,0:T(8,128)(2,1)S(1)}, f32[70,38,256]{2,1,0:T(8,128)S(1)}) fusion(f32[256]{0:T(256)S(1)} %bitcast.212, f32[256]{0:T(256)S(1)} %bitcast.214, f32[256]{0:T(256)S(1)} %bitcast.120, f32[256]{0:T(256)S(1)} %bitcast.122, f32[256]{0:T(256)S(1)} %bitcast.124, f32[256]{0:T(256)S(1)} %bitcast.126, f32[256]{0:T(256)S(1)} %bitcast.128, ...), kind=kLoop, calls=%fused_computation.241 | loop fusion | flops 66734080 | bytes 6233088 | tf_op jit(solution)/shard_map/convert.3
  102.3 0.7 collective-permute-start.6
  103.0 3.8 %collective-permute-start.7 = (bf16[70,3,256]{2,1,0:T(4,128)(2,1)S(1)}, bf16[70,3,256]{2,1,0:T(4,128)(2,1)S(1)}, u32[]{:S(2)}, u32[]{:S(2)}) collective-permute-start(bf16[70,3,256]{2,1,0:T(4,128)(2,1)S(1)} %get-tuple-element.95), channel_id=1, source_target_pairs={{1,0},{2,1},{3,2},{4,3},{5,4},{6,5},{7,6},{8,7},{9,8},{10,9},{11,1... | collective-permute-start | bytes 322568 | tf_op jit(solution)/shard_map/ppermute | solution.py:28
  106.8 4.5 %fusion.122 = f32[256,1024]{1,0:T(8,128)} fusion(bf16[2048,256]{1,0:T(8,128)(2,1)S(1)} %bitcast.114, bf16[2048,1024]{1,0:T(8,128)(2,1)} %copy-done.110), kind=kOutput, calls=%fused_computation.249 | convolution fusion | flops 1073741824 | bytes 6291456 | tf_op jit(solution)/shard_map/dot_general | solution.py:83
  111.3 1.8 slice.866
  113.1 0.6 copy-done.12
  113.7 0.6 copy-done.13
  114.4 1.0 convert_add_fusion.1
  115.4 5.2 %scatter-add.10 = f32[70,32,256]{2,1,0:T(8,128)} dynamic-update-slice(f32[70,32,256]{2,1,0:T(8,128)} %slice.866, f32[70,3,256]{2,1,0:T(4,128)} %convert_add_fusion.1, s32[]{:T(128)} %constant.108.clone.1, s32[]{:T(128)} %constant.108.clone.1, s32[]{:T(128)} %constant.108.clone.1) | dynamic-update-slice | bytes 430084 | tf_op jit(solution)/shard_map/scatter-add | solution.py:126
  120.6 2.1 slice_add_fusion
  122.8 4.6 %scatter-add.11 = f32[70,32,256]{2,1,0:T(8,128)} dynamic-update-slice(f32[70,32,256]{2,1,0:T(8,128)} %scatter-add.10, f32[70,3,256]{2,1,0:T(4,128)} %slice_add_fusion, s32[]{:T(128)} %constant.108.clone.1, s32[]{:T(128)} %constant.109.clone.1, s32[]{:T(128)} %constant.108.clone.1) | dynamic-update-slice | bytes 430084 | tf_op jit(solution)/shard_map/scatter-add | solution.py:127
  127.3 0.9 slice.1409
  128.2 3.2 %maximum_multiply_fusion = f32[256,2048]{1,0:T(8,128)} fusion(f32[256,1024]{1,0:T(8,128)} %fusion.7, f32[256,1024]{1,0:T(8,128)} %fusion.122), kind=kLoop, calls=%fused_computation.162 | loop fusion | flops 1048576 | bytes 4194304 | tf_op jit(solution)/shard_map/mul | solution.py:86
  131.5 6.1 %multiply_reduce_fusion.18 = (f32[256]{0:T(256)S(1)}, f32[256]{0:T(256)S(1)}, f32[256]{0:T(256)S(1)}, f32[256]{0:T(256)S(1)}, f32[256]{0:T(256)S(1)}, /*index=5*...) fusion(f32[64,32,256]{2,1,0:T(8,128)} %copy-done.3, ...), kind=kLoop, calls=%fused_computation.181 | loop fusion | flops 18869760 | bytes 39864320 | tf_op jit(solution)/shard_map/reduce_sum | solution.py:104
  138.0 4.3 %multiply_reduce_fusion.36 = (f32[256]{0:T(256)S(1)}, f32[256]{0:T(256)S(1)}, f32[256]{0:T(256)S(1)}, f32[256]{0:T(256)S(1)}, f32[256]{0:T(256)}, /*index=5*/f32...) fusion(f32[64,32,256]{2,1,0:T(8,128)S(1)} %copy-done.4, ...), kind=kLoop, calls=%fused_computation.199 | loop fusion | flops 13628160 | bytes 29373440 | tf_op jit(solution)/shard_map/reduce_sum | solution.py:104
  142.4 1.6 stack.199
  144.0 1.8 collective-permute-start.11
  145.8 61.8 %psum.7 = f32[7,7,256]{2,1,0:T(8,128)} all-reduce(f32[7,7,256]{2,1,0:T(8,128)S(1)} %mul.1497), channel_id=1, replica_groups=mesh['groups'=2,'lon'=16] {'lon'}, use_global_device_ids=true, to_apply=%region_53.0 | all-reduce | flops 12544 | bytes 100352 | tf_op jit(solution)/shard_map/psum | solution.py:111
  207.6 1.7 slice.871
  209.5 0.9 fusion.108
  210.4 2.5 %fusion.107 = bf16[64,32,256]{2,1,0:T(8,128)(2,1)} fusion(bf16[64,32,256]{2,1,0:T(8,128)(2,1)} %param.16, f32[64,32,256]{2,1,0:T(8,128)S(1)} %fusion.108, f32[64,32]{1,0:T(8,128)S(1)} %copy-done.15), kind=kLoop, calls=%fused_computation.161 | loop fusion | flops 2097152 | bytes 4202496 | tf_op jit(solution)/shard_map/convert_element_type | solution.py:138
  213.0 1.5 fusion.117
  (249 shorter events, 1.5 us)
Async XLA Ops:
  7.2 47.1 %copy-start = (bf16[256,1024]{1,0:T(8,128)(2,1)S(1)}, bf16[256,1024]{1,0:T(8,128)(2,1)}, u32[]{:S(2)}) copy-start(bf16[256,1024]{1,0:T(8,128)(2,1)} %param.19) | copy-start | bytes 1572868
  7.2 205.7 %reduce-scatter.2.cloned.1.call-start = ((), (), s32[]{:S(2)}) async-start(), calls=%async_computation.1 | async-start | bytes 2228224 | tf_op jit(solution)/shard_map/reduce_scatter | solution.py:85
  8.2 10.0 %copy-start.16 = (f32[7,7,256]{2,1,0:T(8,128)S(1)}, f32[7,7,256]{2,1,0:T(8,128)}, u32[]{:S(2)}) copy-start(f32[7,7,256]{2,1,0:T(8,128)} %param.17) | copy-start | bytes 150532
  9.8 23.2 %copy-start.5 = (bf16[64,32,256]{2,1,0:T(8,128)(2,1)}, bf16[64,32,256]{2,1,0:T(8,128)(2,1)S(1)}, u32[]{:S(2)}) copy-start(bf16[64,32,256]{2,1,0:T(8,128)(2,1)S(1)} %broadcast_multiply_fusion) | copy-start | bytes 3145732
  9.8 1.4 collective-permute-start
  10.4 22.6 %copy-start.14 = (f32[64,32]{1,0:T(8,128)}, f32[64,32]{1,0:T(8,128)S(1)}, u32[]{:S(2)}) copy-start(f32[64,32]{1,0:T(8,128)S(1)} %copy.14) | copy-start | bytes 24580
  11.2 4.9 %collective-permute-start.1 = (bf16[3,32,256]{2,1,0:T(8,128)(2,1)S(1)}, bf16[3,32,256]{2,1,0:T(8,128)(2,1)S(1)}, u32[]{:S(2)}, u32[]{:S(2)}) collective-permute-start(bf16[3,32,256]{2,1,0:T(8,128)(2,1)S(1)} %collective-permute-done), channel_id=1, source_target_pairs={{0,2},{2,0},{1,3},{3,1},{4,6},{6,4},{5,7},{7,5},{8,10},{10,8},{9,1... | collective-permute-start | bytes 147464 | tf_op jit(solution)/shard_map/ppermute | solution.py:16
  16.1 4.1 %collective-permute-start.2 = (bf16[3,32,256]{2,1,0:T(8,128)(2,1)S(1)}, bf16[3,32,256]{2,1,0:T(8,128)(2,1)S(1)}, u32[]{:S(2)}, u32[]{:S(2)}) collective-permute-start(bf16[3,32,256]{2,1,0:T(8,128)(2,1)S(1)} %collective-permute-done.1), channel_id=1, source_target_pairs={{0,4},{4,0},{1,5},{5,1},{2,6},{6,2},{3,7},{7,3},{8,12},{12,8},{9,1... | collective-permute-start | bytes 147464 | tf_op jit(solution)/shard_map/ppermute | solution.py:16
  18.2 16.6 %copy-start.18 = (f32[1,1,256]{2,1,0:T(1,128)}, f32[1,1,256]{2,1,0:T(1,128)S(1)}, u32[]{:S(2)}) copy-start(f32[1,1,256]{2,1,0:T(1,128)S(1)} %get-tuple-element.113) | copy-start | bytes 3076
  18.2 16.6 %copy-start.20 = (f32[1,1,256]{2,1,0:T(1,128)}, f32[1,1,256]{2,1,0:T(1,128)S(1)}, u32[]{:S(2)}) copy-start(f32[1,1,256]{2,1,0:T(1,128)S(1)} %get-tuple-element.114) | copy-start | bytes 3076
  18.2 16.6 %copy-start.22 = (f32[1,1,256]{2,1,0:T(1,128)}, f32[1,1,256]{2,1,0:T(1,128)S(1)}, u32[]{:S(2)}) copy-start(f32[1,1,256]{2,1,0:T(1,128)S(1)} %get-tuple-element.115) | copy-start | bytes 3076
  18.2 16.6 %copy-start.24 = (f32[1,1,256]{2,1,0:T(1,128)}, f32[1,1,256]{2,1,0:T(1,128)S(1)}, u32[]{:S(2)}) copy-start(f32[1,1,256]{2,1,0:T(1,128)S(1)} %get-tuple-element.116) | copy-start | bytes 3076
  18.2 16.6 %copy-start.26 = (f32[1,1,256]{2,1,0:T(1,128)}, f32[1,1,256]{2,1,0:T(1,128)S(1)}, u32[]{:S(2)}) copy-start(f32[1,1,256]{2,1,0:T(1,128)S(1)} %get-tuple-element.117) | copy-start | bytes 3076
  18.3 16.6 %copy-start.28 = (f32[1,1,256]{2,1,0:T(1,128)}, f32[1,1,256]{2,1,0:T(1,128)S(1)}, u32[]{:S(2)}) copy-start(f32[1,1,256]{2,1,0:T(1,128)S(1)} %get-tuple-element.118) | copy-start | bytes 3076
  20.3 5.1 %collective-permute-start.3 = (bf16[3,32,256]{2,1,0:T(8,128)(2,1)S(1)}, bf16[3,32,256]{2,1,0:T(8,128)(2,1)S(1)}, u32[]{:S(2)}, u32[]{:S(2)}) collective-permute-start(bf16[3,32,256]{2,1,0:T(8,128)(2,1)S(1)} %collective-permute-done.2), channel_id=1, source_target_pairs={{0,8},{8,0},{1,9},{9,1},{2,10},{10,2},{3,11},{11,3},{4,12},{12,4},... | collective-permute-start | bytes 147464 | tf_op jit(solution)/shard_map/ppermute | solution.py:16
  23.9 11.0 %copy-start.30 = (f32[1,1,256]{2,1,0:T(1,128)}, f32[1,1,256]{2,1,0:T(1,128)S(1)}, u32[]{:S(2)}) copy-start(f32[1,1,256]{2,1,0:T(1,128)S(1)} %get-tuple-element.119) | copy-start | bytes 3076
  23.9 11.0 %copy-start.32 = (f32[1,1,256]{2,1,0:T(1,128)}, f32[1,1,256]{2,1,0:T(1,128)S(1)}, u32[]{:S(2)}) copy-start(f32[1,1,256]{2,1,0:T(1,128)S(1)} %get-tuple-element.120) | copy-start | bytes 3076
  23.9 11.0 %copy-start.34 = (f32[1,1,256]{2,1,0:T(1,128)}, f32[1,1,256]{2,1,0:T(1,128)S(1)}, u32[]{:S(2)}) copy-start(f32[1,1,256]{2,1,0:T(1,128)S(1)} %get-tuple-element.121) | copy-start | bytes 3076
  23.9 11.0 %copy-start.36 = (f32[1,1,256]{2,1,0:T(1,128)}, f32[1,1,256]{2,1,0:T(1,128)S(1)}, u32[]{:S(2)}) copy-start(f32[1,1,256]{2,1,0:T(1,128)S(1)} %get-tuple-element.122) | copy-start | bytes 3076
  23.9 11.0 %copy-start.38 = (f32[1,1,256]{2,1,0:T(1,128)}, f32[1,1,256]{2,1,0:T(1,128)S(1)}, u32[]{:S(2)}) copy-start(f32[1,1,256]{2,1,0:T(1,128)S(1)} %get-tuple-element.123) | copy-start | bytes 3076
  24.0 11.0 %copy-start.40 = (f32[1,1,256]{2,1,0:T(1,128)}, f32[1,1,256]{2,1,0:T(1,128)S(1)}, u32[]{:S(2)}) copy-start(f32[1,1,256]{2,1,0:T(1,128)S(1)} %get-tuple-element.124) | copy-start | bytes 3076
  24.0 11.0 %copy-start.42 = (f32[1,1,256]{2,1,0:T(1,128)}, f32[1,1,256]{2,1,0:T(1,128)S(1)}, u32[]{:S(2)}) copy-start(f32[1,1,256]{2,1,0:T(1,128)S(1)} %get-tuple-element.125) | copy-start | bytes 3076
  24.0 11.0 %copy-start.44 = (f32[1,1,256]{2,1,0:T(1,128)}, f32[1,1,256]{2,1,0:T(1,128)S(1)}, u32[]{:S(2)}) copy-start(f32[1,1,256]{2,1,0:T(1,128)S(1)} %get-tuple-element.126) | copy-start | bytes 3076
  24.0 11.0 %copy-start.46 = (f32[1,1,256]{2,1,0:T(1,128)}, f32[1,1,256]{2,1,0:T(1,128)S(1)}, u32[]{:S(2)}) copy-start(f32[1,1,256]{2,1,0:T(1,128)S(1)} %get-tuple-element.127) | copy-start | bytes 3076
  25.6 7.4 %collective-permute-start.4 = (bf16[70,3,256]{2,1,0:T(4,128)(2,1)S(1)}, bf16[70,3,256]{2,1,0:T(4,128)(2,1)S(1)}, u32[]{:S(2)}, u32[]{:S(2)}) collective-permute-start(bf16[70,3,256]{2,1,0:T(4,128)(2,1)S(1)} %get-tuple-element.96), channel_id=1, source_target_pairs={{0,1},{1,2},{2,3},{3,4},{4,5},{5,6},{6,7},{7,8},{8,9},{9,10},{10,1... | collective-permute-start | bytes 322568 | tf_op jit(solution)/shard_map/ppermute | solution.py:26
  25.6 7.3 %collective-permute-start.5 = (bf16[70,3,256]{2,1,0:T(4,128)(2,1)S(1)}, bf16[70,3,256]{2,1,0:T(4,128)(2,1)S(1)}, u32[]{:S(2)}, u32[]{:S(2)}) collective-permute-start(bf16[70,3,256]{2,1,0:T(4,128)(2,1)S(1)} %get-tuple-element.97), channel_id=1, source_target_pairs={{1,0},{2,1},{3,2},{4,3},{5,4},{6,5},{7,6},{8,7},{9,8},{10,9},{11,1... | collective-permute-start | bytes 322568 | tf_op jit(solution)/shard_map/ppermute | solution.py:28
  72.6 7.0 %copy-start.27 = (f32[1,1,256]{2,1,0:T(1,128)S(1)}, f32[1,1,256]{2,1,0:T(1,128)}, u32[]{:S(2)}) copy-start(f32[1,1,256]{2,1,0:T(1,128)} %copy-done.26) | copy-start | bytes 3076
  72.6 7.0 %copy-start.29 = (f32[1,1,256]{2,1,0:T(1,128)S(1)}, f32[1,1,256]{2,1,0:T(1,128)}, u32[]{:S(2)}) copy-start(f32[1,1,256]{2,1,0:T(1,128)} %copy-done.28) | copy-start | bytes 3076
  72.6 7.0 %copy-start.31 = (f32[1,1,256]{2,1,0:T(1,128)S(1)}, f32[1,1,256]{2,1,0:T(1,128)}, u32[]{:S(2)}) copy-start(f32[1,1,256]{2,1,0:T(1,128)} %copy-done.30) | copy-start | bytes 3076
  72.6 7.0 %copy-start.33 = (f32[1,1,256]{2,1,0:T(1,128)S(1)}, f32[1,1,256]{2,1,0:T(1,128)}, u32[]{:S(2)}) copy-start(f32[1,1,256]{2,1,0:T(1,128)} %copy-done.32) | copy-start | bytes 3076
  72.6 7.0 %copy-start.35 = (f32[1,1,256]{2,1,0:T(1,128)S(1)}, f32[1,1,256]{2,1,0:T(1,128)}, u32[]{:S(2)}) copy-start(f32[1,1,256]{2,1,0:T(1,128)} %copy-done.34) | copy-start | bytes 3076
  72.6 7.0 %copy-start.37 = (f32[1,1,256]{2,1,0:T(1,128)S(1)}, f32[1,1,256]{2,1,0:T(1,128)}, u32[]{:S(2)}) copy-start(f32[1,1,256]{2,1,0:T(1,128)} %copy-done.36) | copy-start | bytes 3076
  72.6 7.0 %copy-start.39 = (f32[1,1,256]{2,1,0:T(1,128)S(1)}, f32[1,1,256]{2,1,0:T(1,128)}, u32[]{:S(2)}) copy-start(f32[1,1,256]{2,1,0:T(1,128)} %copy-done.38) | copy-start | bytes 3076
  72.6 7.0 %copy-start.41 = (f32[1,1,256]{2,1,0:T(1,128)S(1)}, f32[1,1,256]{2,1,0:T(1,128)}, u32[]{:S(2)}) copy-start(f32[1,1,256]{2,1,0:T(1,128)} %copy-done.40) | copy-start | bytes 3076
  72.6 7.0 %copy-start.43 = (f32[1,1,256]{2,1,0:T(1,128)S(1)}, f32[1,1,256]{2,1,0:T(1,128)}, u32[]{:S(2)}) copy-start(f32[1,1,256]{2,1,0:T(1,128)} %copy-done.42) | copy-start | bytes 3076
  72.7 7.0 %copy-start.45 = (f32[1,1,256]{2,1,0:T(1,128)S(1)}, f32[1,1,256]{2,1,0:T(1,128)}, u32[]{:S(2)}) copy-start(f32[1,1,256]{2,1,0:T(1,128)} %copy-done.44) | copy-start | bytes 3076
  72.7 7.0 %copy-start.47 = (f32[1,1,256]{2,1,0:T(1,128)S(1)}, f32[1,1,256]{2,1,0:T(1,128)}, u32[]{:S(2)}) copy-start(f32[1,1,256]{2,1,0:T(1,128)} %copy-done.46) | copy-start | bytes 3076
  72.7 7.0 %copy-start.49 = (f32[1,1,256]{2,1,0:T(1,128)S(1)}, f32[1,1,256]{2,1,0:T(1,128)}, u32[]{:S(2)}) copy-start(f32[1,1,256]{2,1,0:T(1,128)} %get-tuple-element.128) | copy-start | bytes 3076
  72.7 7.0 %copy-start.51 = (f32[1,1,256]{2,1,0:T(1,128)S(1)}, f32[1,1,256]{2,1,0:T(1,128)}, u32[]{:S(2)}) copy-start(f32[1,1,256]{2,1,0:T(1,128)} %get-tuple-element.129) | copy-start | bytes 3076
  79.5 22.6 %copy-start.3 = (f32[64,32,256]{2,1,0:T(8,128)}, f32[64,32,256]{2,1,0:T(8,128)S(1)}, u32[]{:S(2)}) copy-start(f32[64,32,256]{2,1,0:T(8,128)S(1)} %get-tuple-element.89) | copy-start | bytes 6291460
  79.8 26.9 %copy-start.8 = (bf16[64,32,256]{2,1,0:T(8,128)(2,1)S(1)}, bf16[64,32,256]{2,1,0:T(8,128)(2,1)}, u32[]{:S(2)}) copy-start(bf16[64,32,256]{2,1,0:T(8,128)(2,1)} %copy-done.7) | copy-start | bytes 3145732
  102.2 10.8 %copy-start.10 = (bf16[70,3,256]{2,1,0:T(4,128)(2,1)}, bf16[70,3,256]{2,1,0:T(4,128)(2,1)S(1)}, u32[]{:S(2)}) copy-start(bf16[70,3,256]{2,1,0:T(4,128)(2,1)S(1)} %get-tuple-element.95) | copy-start | bytes 322564
  102.3 10.8 %collective-permute-start.6 = (bf16[70,3,256]{2,1,0:T(4,128)(2,1)S(1)}, bf16[70,3,256]{2,1,0:T(4,128)(2,1)S(1)}, u32[]{:S(2)}, u32[]{:S(2)}) collective-permute-start(bf16[70,3,256]{2,1,0:T(4,128)(2,1)S(1)} %get-tuple-element.94), channel_id=1, source_target_pairs={{0,1},{1,2},{2,3},{3,4},{4,5},{5,6},{6,7},{7,8},{8,9},{9,10},{10,1... | collective-permute-start | bytes 322568 | tf_op jit(solution)/shard_map/ppermute | solution.py:26
  103.0 10.1 %collective-permute-start.7 = (bf16[70,3,256]{2,1,0:T(4,128)(2,1)S(1)}, bf16[70,3,256]{2,1,0:T(4,128)(2,1)S(1)}, u32[]{:S(2)}, u32[]{:S(2)}) collective-permute-start(bf16[70,3,256]{2,1,0:T(4,128)(2,1)S(1)} %get-tuple-element.95), channel_id=1, source_target_pairs={{1,0},{2,1},{3,2},{4,3},{5,4},{6,5},{7,6},{8,7},{9,8},{10,9},{11,1... | collective-permute-start | bytes 322568 | tf_op jit(solution)/shard_map/ppermute | solution.py:28
  128.2 3.2 %collective-permute-start.8 = (bf16[3,32,256]{2,1,0:T(8,128)(2,1)S(1)}, bf16[3,32,256]{2,1,0:T(8,128)(2,1)}, u32[]{:S(2)}, u32[]{:S(2)}) collective-permute-start(bf16[3,32,256]{2,1,0:T(8,128)(2,1)S(1)} %slice.1409), channel_id=1, source_target_pairs={{0,1},{1,0},{2,3},{3,2},{4,5},{5,4},{6,7},{7,6},{8,9},{9,8},{10,11... | collective-permute-start | bytes 147464 | tf_op jit(solution)/shard_map/ppermute | solution.py:16
  131.5 6.4 %collective-permute-start.9 = (bf16[3,32,256]{2,1,0:T(8,128)(2,1)}, bf16[3,32,256]{2,1,0:T(8,128)(2,1)}, u32[]{:S(2)}, u32[]{:S(2)}) collective-permute-start(bf16[3,32,256]{2,1,0:T(8,128)(2,1)} %collective-permute-done.8), channel_id=1, source_target_pairs={{0,2},{2,0},{1,3},{3,1},{4,6},{6,4},{5,7},{7,5},{8,10},{10,8},{9,1... | collective-permute-start | bytes 147464 | tf_op jit(solution)/shard_map/ppermute | solution.py:16
  137.9 6.1 %collective-permute-start.10 = (bf16[3,32,256]{2,1,0:T(8,128)(2,1)}, bf16[3,32,256]{2,1,0:T(8,128)(2,1)}, u32[]{:S(2)}, u32[]{:S(2)}) collective-permute-start(bf16[3,32,256]{2,1,0:T(8,128)(2,1)} %collective-permute-done.9), channel_id=1, source_target_pairs={{0,4},{4,0},{1,5},{5,1},{2,6},{6,2},{3,7},{7,3},{8,12},{12,8},{9,1... | collective-permute-start | bytes 147464 | tf_op jit(solution)/shard_map/ppermute | solution.py:16
  144.0 65.4 %collective-permute-start.11 = (bf16[3,32,256]{2,1,0:T(8,128)(2,1)}, bf16[3,32,256]{2,1,0:T(8,128)(2,1)S(1)}, u32[]{:S(2)}, u32[]{:S(2)}) collective-permute-start(bf16[3,32,256]{2,1,0:T(8,128)(2,1)} %collective-permute-done.10), channel_id=1, source_target_pairs={{0,8},{8,0},{1,9},{9,1},{2,10},{10,2},{3,11},{11,3},{4,12},{12,4},... | collective-permute-start | bytes 147464 | tf_op jit(solution)/shard_map/ppermute | solution.py:16
  (76 other events, 390.9 us)
Sparse Core Ops, SparseCore 0:
  131.6 59.5 reduce-scatter.1
where the time goes:
time: 222 us; the launch traced here: 221 us
  other arithmetic  76.8 us (35%)
  blocking collectives  61.8 us (28%)
  local copies, waits for them, and re-layouts  21.1 us (10%)
  starting transfers between devices  19.4 us (9%)
  matrix products  18.8 us (8%)
  between operations  15.8 us (7%)
  waiting for transfers between devices  7.55 us (3%)
    psum x1, blocking collectives, local(): grad_kernel = lax.psum(local_kernel, 'lon')  61.8 us
    another operation x1, other arithmetic  22.2 us
    reduce_sum x3, other arithmetic, local(): jnp.sum(grad_conv * ext_wide[row_tap:row_tap + band_rows, col_tap:col_tap...  17.1 us
    reduce_sum x1, other arithmetic, local(): mean_z = jnp.mean(conv, axis=-1, keepdims=True)  15.9 us
    ppermute x8, starting transfers between devices, from_partner(): return lax.ppermute(block, axis, route)  10.4 us
    ppermute x2, starting transfers between devices, extended_2(): lax.ppermute(head, axis, [((i + 1) % count, i) for i in range(count)])  8.19 us
    dot_general x1, matrix products, local(): dhid = jnp.dot(dout, down_weight, preferred_element_type=jnp.float32)  6.25 us
    scatter-add x1, local copies, waits for them, and re-layouts, local(): grad_padded = grad_padded.at[:, :3].add(arrived[:, :3])  5.24 us
  transfers between devices with their start and end apart: 13, of which 5 were waited for; matrix products, arithmetic and copies ran while one was open for 13% of the time, Pallas kernels for 0%

commit v1 on v0

v1 whole, which is shorter than its diff:
```python
import functools
import math

import jax
import jax.numpy as jnp
from jax import lax
from jax.experimental import pallas as pl
from jax.experimental.pallas import tpu as pltpu
from jax.sharding import PartitionSpec as P

VMEM_LIMIT = 56 * 1024 * 1024
ROOT = math.sqrt(2.0 / math.pi)


def halo(block, count):
    cols = block.shape[1]
    seam = block[block.shape[0] - 3 :]
    left = lax.ppermute(block[:, cols - 3 :], "lon", [(i, (i + 1) % count) for i in range(count)])
    right = lax.ppermute(block[:, :3], "lon", [((i + 1) % count, i) for i in range(count)])
    middle = lax.ppermute(seam, "lon", [(i, count - 1 - i) for i in range(count)])
    before = lax.ppermute(seam[:, :3], "lon", [(i, (count - i) % count) for i in range(count)])
    after = lax.ppermute(
        seam[:, cols - 3 :], "lon", [(i, (2 * count - 2 - i) % count) for i in range(count)]
    )
    ghost = jnp.concatenate([before[:, ::-1], middle[:, ::-1], after[:, ::-1]], axis=1)[::-1]
    return left, right, ghost


def framed(block, left, right, ghost):
    rows, cols, channels = block.shape
    wide = jnp.float32
    body = jnp.concatenate([left.astype(wide), block.astype(wide), right.astype(wide)], axis=1)
    full = jnp.concatenate(
        [jnp.zeros((3, cols + 6, channels), wide), body, ghost.astype(wide)], axis=0
    )
    return jnp.pad(full, ((0, 0), (0, 2), (0, 0)))


def shift_into(source, shifted, rows, cols):
    for col_tap in range(7):

        @pl.loop(0, rows // 2)
        def _(step):
            at = pl.ds(step * 2, 2)
            shifted[col_tap, at] = source[at, col_tap : col_tap + cols, :]


def conv_block(shifted, taps, row, col, lanes, flip):
    total = [jnp.zeros((8, 128), jnp.float32) for _ in range(8)]
    for b in range(7):
        cells = [shifted[b, row + i, pl.ds(col, 8), lanes] for i in range(14)]
        for a in range(7):
            tap = taps[(6 - a) * 7 + 6 - b if flip else a * 7 + b, :, lanes]
            for j in range(8):
                total[j] = total[j] + tap * cells[j + a]
    return total


def forward_kernel(ext, taps, nhat, istd, shifted):
    rows, cols, channels = nhat.shape
    shift_into(ext, shifted, rows + 6, cols)

    @pl.loop(0, (rows // 8) * (cols // 8))
    def _(step):
        row = (step // (cols // 8)) * 8
        col = pl.multiple_of((step % (cols // 8)) * 8, 8)
        halves = [
            conv_block(shifted, taps, row, col, slice(128 * h, 128 * h + 128), False)
            for h in range(channels // 128)
        ]
        for j in range(8):
            parts = [half[j] for half in halves]
            mean = sum(jnp.sum(p, axis=-1, keepdims=True) for p in parts) / channels
            centred = [p - mean for p in parts]
            var = sum(jnp.sum(p * p, axis=-1, keepdims=True) for p in centred) / channels
            inv = lax.rsqrt(var + 1e-06)
            istd[row + j, pl.ds(col, 8), :] = inv
            for h, p in enumerate(centred):
                nhat[row + j, pl.ds(col, 8), 128 * h : 128 * h + 128] = p * inv


def mlp_kernel(
    factor, nhat, istd, mask, cot, gain, scale, up, down, grad, terms, sum_up, sum_down
):
    step = pl.program_id(0)
    hidden_width = up.shape[1]

    @pl.when(step == 0)
    def _():
        sum_up[...] = jnp.zeros_like(sum_up)
        sum_down[...] = jnp.zeros_like(sum_down)

    wide = jnp.float32
    nh = nhat[...]
    normed = (nh * gain[...]).astype(jnp.bfloat16)
    dout = (cot[...].astype(wide) * scale[...] * mask[...]).astype(jnp.bfloat16)
    rows_of = (((0,), (0,)), ((), ()))
    cols_of = (((1,), (1,)), ((), ()))
    dnorm = jnp.zeros(nh.shape, wide)
    part = 512
    for at in range(0, hidden_width, part):
        piece = slice(at, at + part)
        pre = jnp.dot(normed, up[:, piece], preferred_element_type=wide)
        dhid = jnp.dot(dout, down[:, piece], preferred_element_type=wide)
        square = pre * pre
        t = jnp.tanh(pre * (ROOT + (ROOT * 0.044715) * square))
        half = 0.5 + 0.5 * t
        hidden = pre * half
        slope = half + (0.5 * pre) * (1.0 - t * t) * (ROOT + (3.0 * ROOT * 0.044715) * square)
        dpre = (dhid * slope).astype(jnp.bfloat16)
        hidden = hidden.astype(jnp.bfloat16)
        sum_up[:, piece] += lax.dot_general(normed, dpre, rows_of, preferred_element_type=wide)
        sum_down[:, piece] += lax.dot_general(dout, hidden, rows_of, preferred_element_type=wide)
        dnorm += lax.dot_general(dpre, up[:, piece], cols_of, preferred_element_type=wide)
    dn = dnorm * gain[...]
    first = jnp.mean(dn, axis=-1, keepdims=True)
    second = jnp.mean(dn * nh, axis=-1, keepdims=True)
    grad[...] = istd[...] * (dn - first - nh * second)

    @pl.when(step == pl.num_programs(0) - 1)
    def _():
        terms[:, :hidden_width] = (sum_up[...] * factor).astype(terms.dtype)
        terms[:, hidden_width:] = (sum_down[...] * factor).astype(terms.dtype)


def taps_kernel(factor, ext, grad, out, shifted):
    rows, cols, channels = grad.shape
    shift_into(ext, shifted, rows + 6, cols)

    for h in range(channels // 128):
        lanes = slice(128 * h, 128 * h + 128)
        for b in range(7):

            def body(step, total):
                row = step * 8
                total = list(total)
                for col in range(0, cols, 8):
                    there = slice(col, col + 8)
                    cells = [shifted[b, row + i, there, lanes] for i in range(14)]
                    for j in range(8):
                        value = grad[row + j, there, lanes]
                        for a in range(7):
                            total[a] = total[a] + value * cells[j + a]
                return tuple(total)

            start = tuple(jnp.zeros((8, 128), jnp.float32) for _ in range(7))
            total = lax.fori_loop(0, rows // 8, body, start)
            for a in range(7):
                out[a, b : b + 1, lanes] = factor * jnp.sum(total[a], axis=0, keepdims=True)


def back_kernel(gext, taps, mask, cot, out, shifted, summed):
    rows, cols, channels = out.shape
    shift_into(gext, shifted, rows + 6, cols)

    @pl.loop(0, cols // 8)
    def _(step):
        there = pl.ds(pl.multiple_of(step * 8, 8), 8)
        for h in range(channels // 128):
            lanes = slice(128 * h, 128 * h + 128)
            for row in range(rows - 3, rows):
                total = jnp.zeros((8, 128), jnp.float32)
                for a in range(rows + 3 - row, 7):
                    for b in range(7):
                        total = total + taps[a * 7 + b, :, lanes] * shifted[b, row + a, there, lanes]
                summed[row, there, lanes] = total

    shifted[:, rows + 3 :] = jnp.zeros((7, 3, cols, channels), jnp.float32)
    summed[: rows - 3] = jnp.zeros((rows - 3, cols, channels), jnp.float32)

    @pl.loop(0, (rows // 8) * (cols // 8))
    def _(step):
        row = (step // (cols // 8)) * 8
        col = pl.multiple_of((step % (cols // 8)) * 8, 8)
        for h in range(channels // 128):
            lanes = slice(128 * h, 128 * h + 128)
            total = conv_block(shifted, taps, row, col, lanes, True)
            for j in range(8):
                at = summed.at[row + j, pl.ds(col, 8), lanes]
                at[...] = at[...] + total[j]

    @pl.loop(0, rows // 4)
    def _(step):
        at = pl.ds(step * 4, 4)
        out[at] = (cot[at].astype(jnp.float32) + mask[at] * summed[at]).astype(out.dtype)


def local(
    fields, sea_mask, cotangent, depth_kernel, norm_gain, up_weight, down_weight, layer_scale
):
    rows, cols, channels = fields.shape
    count = lax.axis_size("lon")
    cells = rows * cols
    hidden_width = up_weight.shape[1]
    factor = 1.0 / math.sqrt(cells * count)
    wide = jnp.float32
    in_vmem = pl.BlockSpec(memory_space=pltpu.VMEM)
    params = pltpu.CompilerParams(vmem_limit_bytes=VMEM_LIMIT)
    shape = functools.partial(jax.ShapeDtypeStruct, dtype=wide)
    shifted = pltpu.VMEM((7, rows + 6, cols, channels), wide)
    conv_cost = pl.CostEstimate(
        flops=100 * cells * channels, bytes_accessed=12 * cells * channels, transcendentals=0
    )

    masked = fields * sea_mask.astype(jnp.bfloat16)[:, :, None]
    mask = sea_mask.astype(wide)[:, :, None]
    ext = framed(masked, *halo(masked, count))
    taps = jnp.broadcast_to(depth_kernel.reshape(49, 1, channels), (49, 8, channels))

    nhat, istd = pl.pallas_call(
        forward_kernel,
        out_shape=(shape((rows, cols, channels)), shape((rows, cols, 1))),
        in_specs=[in_vmem] * 2,
        out_specs=(in_vmem, in_vmem),
        scratch_shapes=[shifted],
        compiler_params=params,
        cost_estimate=conv_cost,
        name="forward_conv",
    )(ext, taps)

    tile = 256
    by_cell = pl.BlockSpec((tile, channels), lambda i: (i, 0))
    one = pl.BlockSpec((tile, 1), lambda i: (i, 0))
    whole = lambda *dims: pl.BlockSpec(dims, lambda i: (0, 0))
    grad, terms = pl.pallas_call(
        functools.partial(mlp_kernel, factor),
        grid=(cells // tile,),
        out_shape=(
            shape((cells, channels)),
            jax.ShapeDtypeStruct((channels, 2 * hidden_width), jnp.bfloat16),
        ),
        in_specs=[
            by_cell,
            one,
            one,
            by_cell,
            whole(1, channels),
            whole(1, channels),
            whole(channels, hidden_width),
            whole(channels, hidden_width),
        ],
        out_specs=(by_cell, whole(channels, 2 * hidden_width)),
        scratch_shapes=[pltpu.VMEM((channels, hidden_width), wide)] * 2,
        compiler_params=params,
        cost_estimate=pl.CostEstimate(
            flops=10 * cells * channels * hidden_width,
            bytes_accessed=12 * cells * channels,
            transcendentals=cells * hidden_width,
        ),
        name="mlp",
    )(
        nhat.reshape(cells, channels),
        istd.reshape(cells, 1),
        mask.reshape(cells, 1),
        cotangent.reshape(cells, channels),
        norm_gain.reshape(1, channels),
        layer_scale.reshape(1, channels),
        up_weight,
        down_weight,
    )
    grad = grad.reshape(rows, cols, channels)
    around = halo(grad.astype(jnp.bfloat16), count)

    local_kernel = pl.pallas_call(
        functools.partial(taps_kernel, factor),
        out_shape=shape((7, 7, channels)),
        in_specs=[in_vmem] * 2,
        out_specs=in_vmem,
        scratch_shapes=[shifted],
        compiler_params=params,
        cost_estimate=conv_cost,
        name="kernel_grad",
    )(ext, grad)

    grad_fields = pl.pallas_call(
        back_kernel,
        out_shape=jax.ShapeDtypeStruct((rows, cols, channels), jnp.bfloat16),
        in_specs=[in_vmem] * 4,
        out_specs=in_vmem,
        scratch_shapes=[shifted, pltpu.VMEM((rows, cols, channels), wide)],
        compiler_params=params,
        cost_estimate=conv_cost,
        name="back_conv",
    )(framed(grad, *around), taps, mask, cotangent)

    gathered = lax.all_gather(local_kernel, "lon")
    grad_kernel = jnp.sum(gathered, axis=0)
    arrived = lax.all_to_all(
        terms.reshape(count, channels // count, 2 * hidden_width), "lon", 0, 0
    )
    owned = jnp.sum(arrived.astype(wide), axis=0)
    return (grad_fields, grad_kernel, owned[:, :hidden_width], owned[:, hidden_width:])


def solution(mesh):
    return jax.shard_map(
        local,
        mesh=mesh,
        in_specs=(
            P("groups", "lon", None),
            P("groups", "lon"),
            P("groups", "lon", None),
            P(),
            P(),
            P(),
            P(),
            P(),
        ),
        out_specs=(
            P("groups", "lon", None),
            P("groups", None, None),
            P("lon", "groups"),
            P("lon", "groups"),
        ),
        check_vma=False,
    )
```

time: 222 us -> 149 us (0.67)
  other arithmetic: 76.8 us -> 5.87 us
  Pallas kernels: 0 us -> 68.4 us
  blocking collectives: 61.8 us -> 26 us
  matrix products: 18.8 us -> 0 us
  between operations: 15.8 us -> 0.92 us
  starting transfers between devices: 19.4 us -> 33.8 us
  local copies, waits for them, and re-layouts: 21.1 us -> 10.7 us
  waiting for transfers between devices: 7.55 us -> 2.89 us
    pallas_call x0 -> x4, Pallas kernels: none -> 68.4 us  [the longest x1 22.2 us: local(): pl.pallas_call(forward_kernel, out_shape=(shape((rows, cols, channels)),...]
    psum x1 -> x0, blocking collectives: 61.8 us -> none  [local(): grad_kernel = lax.psum(local_kernel, 'lon')]
    reduce_sum x6 -> x2, other arithmetic: 38.2 us -> 2.02 us  [the longest x1 1.87 us: local(): grad_kernel = jnp.sum(gathered, axis=0)]
    all_gather x0 -> x1, blocking collectives: none -> 26 us  [local(): gathered = lax.all_gather(local_kernel, 'lon')]
    another operation x1 -> x0, other arithmetic: 22.2 us -> none
    dot_general x5 -> x0, matrix products: 18.8 us -> none  [the longest x1 6.25 us: local(): dhid = jnp.dot(dout, down_weight, preferred_element_type=jnp.float32)]
    scatter-add x2 -> x0, local copies, waits for them, and re-layouts: 9.82 us -> none  [the longest x1 5.24 us: local(): grad_padded = grad_padded.at[:, :3].add(arrived[:, :3])]
    ppermute x12 -> x10, starting transfers between devices: 19.4 us -> 28.2 us  [the longest x2 17.7 us: halo(): lax.ppermute(seam[:, cols - 3:], 'lon', [(i, (2 * count - 2 - i) % count)...]
  transfers between devices with their start and end apart: 13 -> 11, of which waited for: 5 -> 2; matrix products, arithmetic and copies ran while one was open for 13% -> 7% of each run, Pallas kernels for 0% -> 21%
where the time goes in v1:
time: 149 us
  Pallas kernels  68.4 us (46%)
  starting transfers between devices  33.8 us (23%)
  blocking collectives  26 us (17%)
  local copies, waits for them, and re-layouts  10.7 us (7%)
  other arithmetic  5.87 us (4%)
  waiting for transfers between devices  2.89 us (2%)
    all_gather x1, blocking collectives, local(): gathered = lax.all_gather(local_kernel, 'lon')  26 us
    pallas_call x1, Pallas kernels, local(): pl.pallas_call(forward_kernel, out_shape=(shape((rows, cols, channels)),...  22.2 us
    ppermute x2, starting transfers between devices, halo(): lax.ppermute(seam[:, cols - 3:], 'lon', [(i, (2 * count - 2 - i) % count)...  17.7 us
    pallas_call x1, Pallas kernels, local(): pl.pallas_call(back_kernel, out_shape=jax.ShapeDtypeStruct((rows, cols, c...  17.7 us
    pallas_call x1, Pallas kernels, local(): pl.pallas_call(functools.partial(mlp_kernel, factor), grid=(cells // tile...  15.4 us
    pallas_call x1, Pallas kernels, local(): pl.pallas_call(functools.partial(taps_kernel, factor), out_shape=shape((7...  13 us
    ppermute x2, starting transfers between devices, halo(): lax.ppermute(block[:, :3], 'lon', [((i + 1) % count, i) for i in range(co...  8.47 us
    all_to_all x1, starting transfers between devices, local(): lax.all_to_all(terms.reshape(count, channels // count, 2 * hidden_width),...  5.6 us
  transfers between devices with their start and end apart: 11, of which 2 were waited for; matrix products, arithmetic and copies ran while one was open for 7% of the time, Pallas kernels for 21%

profile of v1, /device:TPU:0, one launch (start us, length us, event | category | flops | bytes accessed | tf_op | source)
XLA Modules:
  0.0 148.5 jit_solution(7817435595855693469)
XLA Ops:
  0.6 0.8 convert_bitcast_fusion
  1.4 0.1 copy.19
  1.5 1.6 %broadcast_multiply_fusion = bf16[64,32,256]{2,1,0:T(8,128)(2,1)S(1)} fusion(bf16[64,32,256]{2,1,0:T(8,128)(2,1)} %param.8, bf16[64,32]{1,0:T(8,128)(2,1)S(1)} %copy.19), kind=kLoop, calls=%fused_computation.4 | loop fusion | flops 524288 | bytes 2101248 | tf_op jit(solution)/shard_map/mul | solution.py:205
  3.1 0.7 collective-permute-start.2
  3.8 9.4 %collective-permute-start.4 = (bf16[3,3,256]{2,1,0:T(4,128)(2,1)S(1)}, bf16[3,3,256]{2,1,0:T(4,128)(2,1)S(1)}, u32[]{:S(2)}, u32[]{:S(2)}) collective-permute-start(bf16[3,3,256]{2,1,0:T(4,128)(2,1)S(1)} %get-tuple-element.19), channel_id=1, source_target_pairs={{0,14},{1,13},{2,12},{3,11},{4,10},{5,9},{6,8},{7,7},{8,6},{9,5},{... | collective-permute-start | bytes 13832 | tf_op jit(solution)/shard_map/ppermute | solution.py:22
  13.2 0.1 collective-permute-start.3
  13.3 0.1 fusion.2
  13.4 0.2 collective-permute-start
  13.6 4.4 %collective-permute-start.1 = (bf16[64,3,256]{2,1,0:T(4,128)(2,1)S(1)}, bf16[64,3,256]{2,1,0:T(4,128)(2,1)S(1)}, u32[]{:S(2)}, u32[]{:S(2)}) collective-permute-start(bf16[64,3,256]{2,1,0:T(4,128)(2,1)S(1)} %get-tuple-element.17), channel_id=1, source_target_pairs={{1,0},{2,1},{3,2},{4,3},{5,4},{6,5},{7,6},{8,7},{9,8},{10,9},{11,1... | collective-permute-start | bytes 294920 | tf_op jit(solution)/shard_map/ppermute | solution.py:19
  17.9 0.1 copy.20
  18.0 2.2 %reshape_broadcast_in_dim.4.mask = f32[2048,1]{1,0:T(8,128)} reshape(f32[64,32]{1,0:T(8,128)S(1)} %copy.20) | data formatting | bytes 16384 | tf_op jit(solution)/shard_map/reshape;broadcast_in_dim | solution.py:254
  20.2 0.0 collective-permute-done.2
  20.2 0.1 rev.24
  20.3 0.0 collective-permute-done.4
  20.3 0.1 rev.26
  20.4 0.1 rev.25
  20.6 0.4 collective-permute-done
  21.0 0.0 collective-permute-done.1
  21.0 0.6 maximum_convert_fusion
  21.5 0.3 pad_maximum_fusion
  21.8 1.8 %pad.7.ext = f32[70,40,256]{2,1,0:T(8,128)} pad(f32[70,38,256]{2,1,0:T(8,128)S(1)} %pad_maximum_fusion, f32[]{:T(128)} %constant.1.clone.1), padding=0_0x0_2x0_0 | pad | bytes 5591044 | tf_op jit(solution)/shard_map/jit(_pad)/pad | solution.py:36
  23.6 0.8 broadcast_in_dim.12.taps
  24.3 22.2 %forward_conv.1 = (f32[64,32,256]{2,1,0:T(8,128)}, f32[64,32,1]{2,1,0:T(8,128)}) custom-call(f32[70,40,256]{2,1,0:T(8,128)} %pad.7.ext, f32[49,8,256]{2,1,0:T(8,128)} %broadcast_in_dim.12.taps), custom_call_target="tpu_custom_call" | custom-call | flops 52428800 | bytes 6291456 | tf_op jit(solution)/shard_map/forward_conv/pallas_call | solution.py:210
  46.6 15.4 %mlp.1 = (f32[2048,256]{1,0:T(8,128)}, bf16[256,2048]{1,0:T(8,128)(2,1)}) custom-call(f32[2048,256]{1,0:T(8,128)} %bitcast.16, f32[2048,1]{1,0:T(8,128)} %bitcast.17, f32[2048,1]{1,0:T(8,128)} %reshape_broadcast_in_dim.4.mask, bf16[2048,256]{1,0:T(8,128)(2,1)} %bitcast.14, f32[1,256]{1,0:T(1,128)} %bitcast.18, f32[1,256]{1,0:T(1,128)} %bitcast.19, ...), custom_call_target="tpu_custom_call" | custom-call | flops 5368709120 | bytes 6291456 | tf_op jit(solution)/shard_map/mlp/pallas_call | solution.py:225
  62.0 5.6 %all-to-all-start = ((bf16[16,16,2048]{2,1,0:T(8,128)(2,1)}), bf16[16,16,2048]{2,1,0:T(8,128)(2,1)S(1)}, u32[]{:S(2)}, u32[]{:S(2)}) async-start(bf16[16,16,2048]{2,1,0:T(8,128)(2,1)} %bitcast.15), calls=%async_computation | async-start | bytes 2097152 | tf_op jit(solution)/shard_map/all_to_all | solution.py:288
  67.6 1.9 %copy.22.mask = f32[64,32,1]{2,1,0:T(8,128)} copy(f32[64,32,1]{0,1,2:T(8,128)S(1)} %get-tuple-element.22) | data formatting | bytes 16384 | tf_op jit(solution)/shard_map/broadcast_in_dim | solution.py:206
  69.5 0.2 convert_element_type.33
  69.7 0.7 collective-permute-start.7
  70.3 8.3 %collective-permute-start.9 = (bf16[3,3,256]{2,1,0:T(4,128)(2,1)S(1)}, bf16[3,3,256]{2,1,0:T(4,128)(2,1)S(1)}, u32[]{:S(2)}, u32[]{:S(2)}) collective-permute-start(bf16[3,3,256]{2,1,0:T(4,128)(2,1)S(1)} %get-tuple-element.15), channel_id=1, source_target_pairs={{0,14},{1,13},{2,12},{3,11},{4,10},{5,9},{6,8},{7,7},{8,6},{9,5},{... | collective-permute-start | bytes 13832 | tf_op jit(solution)/shard_map/ppermute | solution.py:22
  78.7 0.1 collective-permute-start.8
  78.8 13.0 %kernel_grad.1 = f32[7,7,256]{2,1,0:T(8,128)} custom-call(f32[70,40,256]{2,1,0:T(8,128)} %pad.7.ext, f32[64,32,256]{2,1,0:T(8,128)} %bitcast.10), custom_call_target="tpu_custom_call" | custom-call | flops 52428800 | bytes 6291456 | tf_op jit(solution)/shard_map/kernel_grad/pallas_call | solution.py:264
  91.8 26.0 %all-gather = f32[112,7,256]{2,1,0:T(8,128)} all-gather(f32[7,7,256]{2,1,0:T(8,128)} %kernel_grad.1), channel_id=2, replica_groups=mesh['groups'=2,'lon'=16] {'lon'}, dimensions={0}, use_global_device_ids=true | all-gather | bytes 852992 | tf_op jit(solution)/shard_map/all_gather | solution.py:286
  117.8 0.8 fusion
  118.6 1.9 %reduce_sum.18 = f32[7,7,256]{2,1,0:T(8,128)} reduce(f32[16,7,7,256]{3,2,1,0:T(8,128)} %bitcast.13, f32[]{:T(128)} %constant.1.clone.1), dimensions={0}, to_apply=%region_0.1 | reduce | flops 188160 | bytes 852996 | tf_op jit(solution)/shard_map/reduce_sum | solution.py:287
  120.5 0.4 collective-permute-start.5
  120.8 4.1 %collective-permute-start.6 = (bf16[64,3,256]{2,1,0:T(4,128)(2,1)}, bf16[64,3,256]{2,1,0:T(4,128)(2,1)S(1)}, u32[]{:S(2)}, u32[]{:S(2)}) collective-permute-start(bf16[64,3,256]{2,1,0:T(4,128)(2,1)} %get-tuple-element.13), channel_id=1, source_target_pairs={{1,0},{2,1},{3,2},{4,3},{5,4},{6,5},{7,6},{8,7},{9,8},{10,9},{11,1... | collective-permute-start | bytes 294920 | tf_op jit(solution)/shard_map/ppermute | solution.py:19
  124.9 0.1 rev.28
  125.0 0.0 collective-permute-done.9
  125.0 0.1 rev.30
  125.1 0.0 collective-permute-done.8
  125.1 0.1 rev.29
  125.3 2.5 %collective-permute-done.5 = bf16[64,3,256]{2,1,0:T(4,128)(2,1)S(1)} collective-permute-done((bf16[64,3,256]{2,1,0:T(4,128)(2,1)}, bf16[64,3,256]{2,1,0:T(4,128)(2,1)S(1)}, u32[]{:S(2)}, u32[]{:S(2)}) %collective-permute-start.5) | collective-permute-done | bytes 98336 | tf_op jit(solution)/shard_map/ppermute | solution.py:18
  127.8 0.4 pad_maximum_fusion.1
  128.2 1.8 %pad.8.gext = f32[70,40,256]{2,1,0:T(8,128)} pad(f32[70,38,256]{2,1,0:T(8,128)S(1)} %pad_maximum_fusion.1, f32[]{:T(128)} %constant.1.clone.1), padding=0_0x0_2x0_0 | pad | bytes 5591044 | tf_op jit(solution)/shard_map/jit(_pad)/pad | solution.py:36
  130.0 17.7 %back_conv.1 = bf16[64,32,256]{2,1,0:T(8,128)(2,1)} custom-call(f32[70,40,256]{2,1,0:T(8,128)} %pad.8.gext, f32[49,8,256]{2,1,0:T(8,128)} %broadcast_in_dim.12.taps, f32[64,32,1]{2,1,0:T(8,128)} %copy.22.mask, bf16[64,32,256]{2,1,0:T(8,128)(2,1)} %cot.1), custom_call_target="tpu_custom_call" | custom-call | flops 52428800 | bytes 6291456 | tf_op jit(solution)/shard_map/back_conv/pallas_call | solution.py:275
  147.7 0.0 all-to-all-done
  147.7 0.1 convert_reduce_fusion
  147.9 0.7 fusion.4
  (22 shorter events, 0.2 us)
Async XLA Ops:
  0.6 17.3 %copy-start.2 = (f32[7,7,256]{2,1,0:T(8,128)S(1)}, f32[7,7,256]{2,1,0:T(8,128)}, u32[]{:S(2)}) copy-start(f32[7,7,256]{2,1,0:T(8,128)} %param.11) | copy-start | bytes 150532
  3.1 17.1 %collective-permute-start.2 = (bf16[3,3,256]{2,1,0:T(4,128)(2,1)S(1)}, bf16[3,3,256]{2,1,0:T(4,128)(2,1)S(1)}, u32[]{:S(2)}, u32[]{:S(2)}) collective-permute-start(bf16[3,3,256]{2,1,0:T(4,128)(2,1)S(1)} %get-tuple-element.18), channel_id=1, source_target_pairs={{0,0},{1,15},{2,14},{3,13},{4,12},{5,11},{6,10},{7,9},{8,8},{9,7},... | collective-permute-start | bytes 13832 | tf_op jit(solution)/shard_map/ppermute | solution.py:21
  3.8 16.5 %collective-permute-start.4 = (bf16[3,3,256]{2,1,0:T(4,128)(2,1)S(1)}, bf16[3,3,256]{2,1,0:T(4,128)(2,1)S(1)}, u32[]{:S(2)}, u32[]{:S(2)}) collective-permute-start(bf16[3,3,256]{2,1,0:T(4,128)(2,1)S(1)} %get-tuple-element.19), channel_id=1, source_target_pairs={{0,14},{1,13},{2,12},{3,11},{4,10},{5,9},{6,8},{7,7},{8,6},{9,5},{... | collective-permute-start | bytes 13832 | tf_op jit(solution)/shard_map/ppermute | solution.py:22
  13.2 7.2 %collective-permute-start.3 = (bf16[3,32,256]{2,1,0:T(8,128)(2,1)S(1)}, bf16[3,32,256]{2,1,0:T(8,128)(2,1)S(1)}, u32[]{:S(2)}, u32[]{:S(2)}) collective-permute-start(bf16[3,32,256]{2,1,0:T(8,128)(2,1)S(1)} %slice.55), channel_id=1, source_target_pairs={{0,15},{1,14},{2,13},{3,12},{4,11},{5,10},{6,9},{7,8},{8,7},{9,6},... | collective-permute-start | bytes 147464 | tf_op jit(solution)/shard_map/ppermute | solution.py:20
  13.4 7.6 %collective-permute-start = (bf16[64,3,256]{2,1,0:T(4,128)(2,1)S(1)}, bf16[64,3,256]{2,1,0:T(4,128)(2,1)S(1)}, u32[]{:S(2)}, u32[]{:S(2)}) collective-permute-start(bf16[64,3,256]{2,1,0:T(4,128)(2,1)S(1)} %get-tuple-element.16), channel_id=1, source_target_pairs={{0,1},{1,2},{2,3},{3,4},{4,5},{5,6},{6,7},{7,8},{8,9},{9,10},{10,1... | collective-permute-start | bytes 294920 | tf_op jit(solution)/shard_map/ppermute | solution.py:18
  13.6 7.4 %collective-permute-start.1 = (bf16[64,3,256]{2,1,0:T(4,128)(2,1)S(1)}, bf16[64,3,256]{2,1,0:T(4,128)(2,1)S(1)}, u32[]{:S(2)}, u32[]{:S(2)}) collective-permute-start(bf16[64,3,256]{2,1,0:T(4,128)(2,1)S(1)} %get-tuple-element.17), channel_id=1, source_target_pairs={{1,0},{2,1},{3,2},{4,3},{5,4},{6,5},{7,6},{8,7},{9,8},{10,9},{11,1... | collective-permute-start | bytes 294920 | tf_op jit(solution)/shard_map/ppermute | solution.py:19
  62.0 7.5 %copy-start = (f32[2048,256]{1,0:T(8,128)S(1)}, f32[2048,256]{1,0:T(8,128)}, u32[]{:S(2)}) copy-start(f32[2048,256]{1,0:T(8,128)} %get-tuple-element.10) | copy-start | bytes 6291460
  62.0 85.7 %all-to-all-start = ((bf16[16,16,2048]{2,1,0:T(8,128)(2,1)}), bf16[16,16,2048]{2,1,0:T(8,128)(2,1)S(1)}, u32[]{:S(2)}, u32[]{:S(2)}) async-start(bf16[16,16,2048]{2,1,0:T(8,128)(2,1)} %bitcast.15), calls=%async_computation | async-start | bytes 2097152 | tf_op jit(solution)/shard_map/all_to_all | solution.py:288
  69.7 55.2 %collective-permute-start.7 = (bf16[3,3,256]{2,1,0:T(4,128)(2,1)S(1)}, bf16[3,3,256]{2,1,0:T(4,128)(2,1)S(1)}, u32[]{:S(2)}, u32[]{:S(2)}) collective-permute-start(bf16[3,3,256]{2,1,0:T(4,128)(2,1)S(1)} %get-tuple-element.14), channel_id=1, source_target_pairs={{0,0},{1,15},{2,14},{3,13},{4,12},{5,11},{6,10},{7,9},{8,8},{9,7},... | collective-permute-start | bytes 13832 | tf_op jit(solution)/shard_map/ppermute | solution.py:21
  70.3 54.6 %collective-permute-start.9 = (bf16[3,3,256]{2,1,0:T(4,128)(2,1)S(1)}, bf16[3,3,256]{2,1,0:T(4,128)(2,1)S(1)}, u32[]{:S(2)}, u32[]{:S(2)}) collective-permute-start(bf16[3,3,256]{2,1,0:T(4,128)(2,1)S(1)} %get-tuple-element.15), channel_id=1, source_target_pairs={{0,14},{1,13},{2,12},{3,11},{4,10},{5,9},{6,8},{7,7},{8,6},{9,5},{... | collective-permute-start | bytes 13832 | tf_op jit(solution)/shard_map/ppermute | solution.py:22
  78.7 46.4 %collective-permute-start.8 = (bf16[3,32,256]{2,1,0:T(8,128)(2,1)S(1)}, bf16[3,32,256]{2,1,0:T(8,128)(2,1)S(1)}, u32[]{:S(2)}, u32[]{:S(2)}) collective-permute-start(bf16[3,32,256]{2,1,0:T(8,128)(2,1)S(1)} %slice.60), channel_id=1, source_target_pairs={{0,15},{1,14},{2,13},{3,12},{4,11},{5,10},{6,9},{7,8},{8,7},{9,6},... | collective-permute-start | bytes 147464 | tf_op jit(solution)/shard_map/ppermute | solution.py:20
  91.8 36.0 %copy-start.1 = (f32[2048,256]{1,0:T(8,128)S(1)}, f32[2048,256]{1,0:T(8,128)}, u32[]{:S(2)}) copy-start(f32[2048,256]{1,0:T(8,128)} %get-tuple-element.10) | copy-start | bytes 6291460
  120.5 7.3 %collective-permute-start.5 = (bf16[64,3,256]{2,1,0:T(4,128)(2,1)}, bf16[64,3,256]{2,1,0:T(4,128)(2,1)S(1)}, u32[]{:S(2)}, u32[]{:S(2)}) collective-permute-start(bf16[64,3,256]{2,1,0:T(4,128)(2,1)} %get-tuple-element.12), channel_id=1, source_target_pairs={{0,1},{1,2},{2,3},{3,4},{4,5},{5,6},{6,7},{7,8},{8,9},{9,10},{10,1... | collective-permute-start | bytes 294920 | tf_op jit(solution)/shard_map/ppermute | solution.py:18
  120.8 7.0 %collective-permute-start.6 = (bf16[64,3,256]{2,1,0:T(4,128)(2,1)}, bf16[64,3,256]{2,1,0:T(4,128)(2,1)S(1)}, u32[]{:S(2)}, u32[]{:S(2)}) collective-permute-start(bf16[64,3,256]{2,1,0:T(4,128)(2,1)} %get-tuple-element.13), channel_id=1, source_target_pairs={{1,0},{2,1},{3,2},{4,3},{5,4},{6,5},{7,6},{8,7},{9,8},{10,9},{11,1... | collective-permute-start | bytes 294920 | tf_op jit(solution)/shard_map/ppermute | solution.py:19

commit v2 on v1

--- a/solution.py
+++ b/solution.py
@@ -17,12 +17,8 @@
     seam = block[block.shape[0] - 3 :]
     left = lax.ppermute(block[:, cols - 3 :], "lon", [(i, (i + 1) % count) for i in range(count)])
     right = lax.ppermute(block[:, :3], "lon", [((i + 1) % count, i) for i in range(count)])
-    middle = lax.ppermute(seam, "lon", [(i, count - 1 - i) for i in range(count)])
-    before = lax.ppermute(seam[:, :3], "lon", [(i, (count - i) % count) for i in range(count)])
-    after = lax.ppermute(
-        seam[:, cols - 3 :], "lon", [(i, (2 * count - 2 - i) % count) for i in range(count)]
-    )
-    ghost = jnp.concatenate([before[:, ::-1], middle[:, ::-1], after[:, ::-1]], axis=1)[::-1]
+    seam = jnp.concatenate([left[-3:], seam, right[-3:]], axis=1)
+    ghost = lax.ppermute(seam, "lon", [(i, count - 1 - i) for i in range(count)])[::-1, ::-1]
     return left, right, ghost
 
 
@@ -283,6 +279,7 @@
         name="back_conv",
     )(framed(grad, *around), taps, mask, cotangent)
 
+    local_kernel, grad_fields = lax.optimization_barrier((local_kernel, grad_fields))
     gathered = lax.all_gather(local_kernel, "lon")
     grad_kernel = jnp.sum(gathered, axis=0)
     arrived = lax.all_to_all(

time: 149 us -> 155 us (1.040)
  waiting for transfers between devices: 2.89 us -> 28.4 us
  starting transfers between devices: 33.8 us -> 14.2 us
  blocking collectives: 26 us -> 23.5 us
  other arithmetic: 5.87 us -> 8.17 us
    ppermute x4 -> x0, starting transfers between devices: 19 us -> none  [the longest x2 17.7 us: halo(): lax.ppermute(seam[:, cols - 3:], 'lon', [(i, (2 * count - 2 - i) % count)...]
    ppermute x2, waiting for transfers between devices: 0.01 us -> 15.3 us  [halo(): lax.ppermute(block[:, :3], 'lon', [((i + 1) % count, i) for i in range(co...]
    ppermute x2, waiting for transfers between devices: 2.86 us -> 9 us  [halo(): lax.ppermute(block[:, cols - 3:], 'lon', [(i, (i + 1) % count) for i in r...]
    ppermute x2, waiting for transfers between devices: 0.01 us -> 4.1 us  [halo(): lax.ppermute(seam, 'lon', [(i, count - 1 - i) for i in range(count)])]
    all_gather x1, blocking collectives: 26 us -> 23.5 us  [local(): gathered = lax.all_gather(local_kernel, 'lon')]
    all_to_all x1, starting transfers between devices: 5.6 us -> 3.8 us  [local(): lax.all_to_all(terms.reshape(count, channels // count, 2 * hidden_width),...]
  transfers between devices with their start and end apart: 11 -> 7, of which waited for: 2 -> 4; matrix products, arithmetic and copies ran while one was open for 7% -> 8% of each run, Pallas kernels for 21% -> 20%
where the time goes in v2:
time: 155 us
  Pallas kernels  68.5 us (44%)
  waiting for transfers between devices  28.4 us (18%)
  blocking collectives  23.5 us (15%)
  starting transfers between devices  14.2 us (9%)
  local copies, waits for them, and re-layouts  11.2 us (7%)
  other arithmetic  8.17 us (5%)
    all_gather x1, blocking collectives, local(): gathered = lax.all_gather(local_kernel, 'lon')  23.5 us
    pallas_call x1, Pallas kernels, local(): pl.pallas_call(forward_kernel, out_shape=(shape((rows, cols, channels)),...  22.2 us
    pallas_call x1, Pallas kernels, local(): pl.pallas_call(back_kernel, out_shape=jax.ShapeDtypeStruct((rows, cols, c...  17.7 us
    pallas_call x1, Pallas kernels, local(): pl.pallas_call(functools.partial(mlp_kernel, factor), grid=(cells // tile...  15.4 us
    ppermute x2, waiting for transfers between devices, halo(): lax.ppermute(block[:, :3], 'lon', [((i + 1) % count, i) for i in range(co...  15.3 us
    pallas_call x1, Pallas kernels, local(): pl.pallas_call(functools.partial(taps_kernel, factor), out_shape=shape((7...  13.2 us
    ppermute x2, starting transfers between devices, halo(): lax.ppermute(block[:, :3], 'lon', [((i + 1) % count, i) for i in range(co...  9.89 us
    ppermute x2, waiting for transfers between devices, halo(): lax.ppermute(block[:, cols - 3:], 'lon', [(i, (i + 1) % count) for i in r...  9 us
  transfers between devices with their start and end apart: 7, of which 4 were waited for; matrix products, arithmetic and copies ran while one was open for 8% of the time, Pallas kernels for 20%

profile of v2, /device:TPU:0, one launch (start us, length us, event | category | flops | bytes accessed | tf_op | source)
XLA Modules:
  0.0 154.8 jit_solution(6123087599964244173)
XLA Ops:
  0.6 0.8 convert_bitcast_fusion
  1.4 0.1 copy.19
  1.5 1.6 %broadcast_multiply_fusion = bf16[64,32,256]{2,1,0:T(8,128)(2,1)S(1)} fusion(bf16[64,32,256]{2,1,0:T(8,128)(2,1)} %param.8, bf16[64,32]{1,0:T(8,128)(2,1)S(1)} %copy.19), kind=kLoop, calls=%fused_computation.4 | loop fusion | flops 524288 | bytes 2101248 | tf_op jit(solution)/shard_map/mul | solution.py:201
  3.1 0.0 copy-start.2
  3.1 0.1 fusion.1
  3.2 5.5 %collective-permute-start.1 = (bf16[64,3,256]{2,1,0:T(4,128)(2,1)S(1)}, bf16[64,3,256]{2,1,0:T(4,128)(2,1)S(1)}, u32[]{:S(2)}, u32[]{:S(2)}) collective-permute-start(bf16[64,3,256]{2,1,0:T(4,128)(2,1)S(1)} %get-tuple-element.19), channel_id=1, source_target_pairs={{1,0},{2,1},{3,2},{4,3},{5,4},{6,5},{7,6},{8,7},{9,8},{10,9},{11,1... | collective-permute-start | bytes 294920 | tf_op jit(solution)/shard_map/ppermute | solution.py:19
  8.7 0.0 collective-permute-start
  8.7 0.0 copy-done.2
  8.7 0.8 broadcast_in_dim.11
  9.6 0.1 copy.20
  9.6 2.2 %reshape_broadcast_in_dim.4.mask = f32[2048,1]{1,0:T(8,128)} reshape(f32[64,32]{1,0:T(8,128)S(1)} %copy.20) | data formatting | bytes 16384 | tf_op jit(solution)/shard_map/reshape;broadcast_in_dim | solution.py:250
  11.8 0.0 collective-permute-done.1
  11.8 4.0 %collective-permute-done = bf16[64,3,256]{2,1,0:T(4,128)(2,1)S(1)} collective-permute-done((bf16[64,3,256]{2,1,0:T(4,128)(2,1)S(1)}, bf16[64,3,256]{2,1,0:T(4,128)(2,1)S(1)}, u32[]{:S(2)}, u32[]{:S(2)}) %collective-permute-start) | collective-permute-done | bytes 98336 | tf_op jit(solution)/shard_map/ppermute | solution.py:18
  15.8 0.5 collective-permute-start.2
  16.4 1.8 %maximum_convert_fusion = f32[64,38,256]{2,1,0:T(8,128)S(1)} fusion(bf16[64,3,256]{2,1,0:T(4,128)(2,1)S(1)} %collective-permute-done.1, bf16[64,32,256]{2,1,0:T(8,128)(2,1)} %copy-done.2, bf16[64,3,256]{2,1,0:T(4,128)(2,1)S(1)} %collective-permute-done), kind=kLoop, calls=%fused_computation.3 | loop fusion | flops 3735552 | bytes 3735552 | tf_op jit(solution)/shard_map/concatenate | solution.py:28
  18.2 4.1 %collective-permute-done.2 = bf16[3,38,256]{2,1,0:T(8,128)(2,1)S(1)} collective-permute-done((bf16[3,38,256]{2,1,0:T(8,128)(2,1)S(1)}, bf16[3,38,256]{2,1,0:T(8,128)(2,1)S(1)}, u32[]{:S(2)}, u32[]{:S(2)}) %collective-permute-start.2) | collective-permute-done | bytes 58400 | tf_op jit(solution)/shard_map/ppermute | solution.py:21
  22.3 0.1 rev.6
  22.4 0.3 pad_maximum_fusion
  22.6 1.8 %pad.7.ext = f32[70,40,256]{2,1,0:T(8,128)} pad(f32[70,38,256]{2,1,0:T(8,128)S(1)} %pad_maximum_fusion, f32[]{:T(128)} %constant.1.clone.1), padding=0_0x0_2x0_0 | pad | bytes 5591044 | tf_op jit(solution)/shard_map/jit(_pad)/pad | solution.py:32
  24.4 0.8 broadcast_in_dim.12.taps
  25.2 22.2 %forward_conv.1 = (f32[64,32,256]{2,1,0:T(8,128)}, f32[64,32,1]{2,1,0:T(8,128)}) custom-call(f32[70,40,256]{2,1,0:T(8,128)} %pad.7.ext, f32[49,8,256]{2,1,0:T(8,128)} %broadcast_in_dim.12.taps), custom_call_target="tpu_custom_call" | custom-call | flops 52428800 | bytes 6291456 | tf_op jit(solution)/shard_map/forward_conv/pallas_call | solution.py:206
  47.4 15.4 %mlp.1 = (f32[2048,256]{1,0:T(8,128)}, bf16[256,2048]{1,0:T(8,128)(2,1)}) custom-call(f32[2048,256]{1,0:T(8,128)} %bitcast.16, f32[2048,1]{1,0:T(8,128)} %bitcast.17, f32[2048,1]{1,0:T(8,128)} %reshape_broadcast_in_dim.4.mask, bf16[2048,256]{1,0:T(8,128)(2,1)} %bitcast.14, f32[1,256]{1,0:T(1,128)} %bitcast.18, f32[1,256]{1,0:T(1,128)} %bitcast.19, ...), custom_call_target="tpu_custom_call" | custom-call | flops 5368709120 | bytes 6291456 | tf_op jit(solution)/shard_map/mlp/pallas_call | solution.py:221
  62.9 3.8 %all-to-all-start = ((bf16[16,16,2048]{2,1,0:T(8,128)(2,1)}), bf16[16,16,2048]{2,1,0:T(8,128)(2,1)S(1)}, u32[]{:S(2)}, u32[]{:S(2)}) async-start(bf16[16,16,2048]{2,1,0:T(8,128)(2,1)} %bitcast.15), calls=%async_computation | async-start | bytes 2097152 | tf_op jit(solution)/shard_map/all_to_all | solution.py:285
  66.7 0.0 copy-done
  66.7 0.2 convert_element_type.33
  66.9 0.1 fusion
  67.0 4.4 %collective-permute-start.4 = (bf16[64,3,256]{2,1,0:T(4,128)(2,1)S(1)}, bf16[64,3,256]{2,1,0:T(4,128)(2,1)S(1)}, u32[]{:S(2)}, u32[]{:S(2)}) collective-permute-start(bf16[64,3,256]{2,1,0:T(4,128)(2,1)S(1)} %get-tuple-element.17), channel_id=1, source_target_pairs={{1,0},{2,1},{3,2},{4,3},{5,4},{6,5},{7,6},{8,7},{9,8},{10,9},{11,1... | collective-permute-start | bytes 294920 | tf_op jit(solution)/shard_map/ppermute | solution.py:19
  71.4 0.0 collective-permute-start.3
  71.4 15.3 %collective-permute-done.4 = bf16[64,3,256]{2,1,0:T(4,128)(2,1)S(1)} collective-permute-done((bf16[64,3,256]{2,1,0:T(4,128)(2,1)S(1)}, bf16[64,3,256]{2,1,0:T(4,128)(2,1)S(1)}, u32[]{:S(2)}, u32[]{:S(2)}) %collective-permute-start.4) | collective-permute-done | bytes 98336 | tf_op jit(solution)/shard_map/ppermute | solution.py:19
  86.6 5.0 %collective-permute-done.3 = bf16[64,3,256]{2,1,0:T(4,128)(2,1)S(1)} collective-permute-done((bf16[64,3,256]{2,1,0:T(4,128)(2,1)S(1)}, bf16[64,3,256]{2,1,0:T(4,128)(2,1)S(1)}, u32[]{:S(2)}, u32[]{:S(2)}) %collective-permute-start.3) | collective-permute-done | bytes 98336 | tf_op jit(solution)/shard_map/ppermute | solution.py:18
  91.7 0.7 pad_maximum_fusion.3
  92.3 0.0 collective-permute-start.5
  92.3 0.0 copy-done.4
  92.3 1.8 %copy.22.mask = f32[64,32,1]{2,1,0:T(8,128)} copy(f32[64,32,1]{0,1,2:T(8,128)S(1)} %get-tuple-element.22) | data formatting | bytes 16384 | tf_op jit(solution)/shard_map/broadcast_in_dim | solution.py:202
  94.2 13.2 %kernel_grad.1 = f32[7,7,256]{2,1,0:T(8,128)} custom-call(f32[70,40,256]{2,1,0:T(8,128)} %pad.7.ext, f32[64,32,256]{2,1,0:T(8,128)} %bitcast.10), custom_call_target="tpu_custom_call" | custom-call | flops 52428800 | bytes 6291456 | tf_op jit(solution)/shard_map/kernel_grad/pallas_call | solution.py:260
  107.4 0.0 copy-done.5
  107.4 0.7 convert_element_type.34
  108.1 0.0 collective-permute-done.5
  108.1 0.8 rev.7
  109.0 0.0 copy-done.1
  109.0 1.3 pad_maximum_fusion.1
  110.3 1.8 %pad.8.gext = f32[70,40,256]{2,1,0:T(8,128)} pad(f32[70,38,256]{2,1,0:T(8,128)S(1)} %pad_maximum_fusion.1, f32[]{:T(128)} %constant.1.clone.1), padding=0_0x0_2x0_0 | pad | bytes 5591044 | tf_op jit(solution)/shard_map/jit(_pad)/pad | solution.py:32
  112.1 17.7 %back_conv.1 = bf16[64,32,256]{2,1,0:T(8,128)(2,1)} custom-call(f32[70,40,256]{2,1,0:T(8,128)} %pad.8.gext, f32[49,8,256]{2,1,0:T(8,128)} %broadcast_in_dim.12.taps, f32[64,32,1]{2,1,0:T(8,128)} %copy.22.mask, bf16[64,32,256]{2,1,0:T(8,128)(2,1)} %cot.1), custom_call_target="tpu_custom_call" | custom-call | flops 52428800 | bytes 6291456 | tf_op jit(solution)/shard_map/back_conv/pallas_call | solution.py:271
  129.8 23.5 %all-gather = f32[112,7,256]{2,1,0:T(8,128)S(1)} all-gather(f32[7,7,256]{2,1,0:T(8,128)S(1)} %copy-done.3), channel_id=2, replica_groups=mesh['groups'=2,'lon'=16] {'lon'}, dimensions={0}, use_global_device_ids=true | all-gather | bytes 852992 | tf_op jit(solution)/shard_map/all_gather | solution.py:283
  153.3 0.7 reduce_sum.18
  154.0 0.0 all-to-all-done
  154.0 0.1 convert_reduce_fusion
  154.2 0.7 fusion.2
  (18 shorter events, 0.1 us)
Async XLA Ops:
  3.1 5.6 %copy-start.2 = (bf16[64,32,256]{2,1,0:T(8,128)(2,1)}, bf16[64,32,256]{2,1,0:T(8,128)(2,1)S(1)}, u32[]{:S(2)}) copy-start(bf16[64,32,256]{2,1,0:T(8,128)(2,1)S(1)} %broadcast_multiply_fusion) | copy-start | bytes 3145732
  3.2 8.6 %collective-permute-start.1 = (bf16[64,3,256]{2,1,0:T(4,128)(2,1)S(1)}, bf16[64,3,256]{2,1,0:T(4,128)(2,1)S(1)}, u32[]{:S(2)}, u32[]{:S(2)}) collective-permute-start(bf16[64,3,256]{2,1,0:T(4,128)(2,1)S(1)} %get-tuple-element.19), channel_id=1, source_target_pairs={{1,0},{2,1},{3,2},{4,3},{5,4},{6,5},{7,6},{8,7},{9,8},{10,9},{11,1... | collective-permute-start | bytes 294920 | tf_op jit(solution)/shard_map/ppermute | solution.py:19
  8.7 7.1 %collective-permute-start = (bf16[64,3,256]{2,1,0:T(4,128)(2,1)S(1)}, bf16[64,3,256]{2,1,0:T(4,128)(2,1)S(1)}, u32[]{:S(2)}, u32[]{:S(2)}) collective-permute-start(bf16[64,3,256]{2,1,0:T(4,128)(2,1)S(1)} %get-tuple-element.18), channel_id=1, source_target_pairs={{0,1},{1,2},{2,3},{3,4},{4,5},{5,6},{6,7},{7,8},{8,9},{9,10},{10,1... | collective-permute-start | bytes 294920 | tf_op jit(solution)/shard_map/ppermute | solution.py:18
  15.8 6.4 %collective-permute-start.2 = (bf16[3,38,256]{2,1,0:T(8,128)(2,1)S(1)}, bf16[3,38,256]{2,1,0:T(8,128)(2,1)S(1)}, u32[]{:S(2)}, u32[]{:S(2)}) collective-permute-start(bf16[3,38,256]{2,1,0:T(8,128)(2,1)S(1)} %pad_maximum_fusion.2), channel_id=1, source_target_pairs={{0,15},{1,14},{2,13},{3,12},{4,11},{5,10},{6,9},{7,8},{8,7},{9,6},... | collective-permute-start | bytes 175112 | tf_op jit(solution)/shard_map/ppermute | solution.py:21
  62.9 3.8 %copy-start = (f32[2048,256]{1,0:T(8,128)S(1)}, f32[2048,256]{1,0:T(8,128)}, u32[]{:S(2)}) copy-start(f32[2048,256]{1,0:T(8,128)} %get-tuple-element.12) | copy-start | bytes 6291460
  62.9 91.1 %all-to-all-start = ((bf16[16,16,2048]{2,1,0:T(8,128)(2,1)}), bf16[16,16,2048]{2,1,0:T(8,128)(2,1)S(1)}, u32[]{:S(2)}, u32[]{:S(2)}) async-start(bf16[16,16,2048]{2,1,0:T(8,128)(2,1)} %bitcast.15), calls=%async_computation | async-start | bytes 2097152 | tf_op jit(solution)/shard_map/all_to_all | solution.py:285
  67.0 19.7 %collective-permute-start.4 = (bf16[64,3,256]{2,1,0:T(4,128)(2,1)S(1)}, bf16[64,3,256]{2,1,0:T(4,128)(2,1)S(1)}, u32[]{:S(2)}, u32[]{:S(2)}) collective-permute-start(bf16[64,3,256]{2,1,0:T(4,128)(2,1)S(1)} %get-tuple-element.17), channel_id=1, source_target_pairs={{1,0},{2,1},{3,2},{4,3},{5,4},{6,5},{7,6},{8,7},{9,8},{10,9},{11,1... | collective-permute-start | bytes 294920 | tf_op jit(solution)/shard_map/ppermute | solution.py:19
  71.4 20.3 %collective-permute-start.3 = (bf16[64,3,256]{2,1,0:T(4,128)(2,1)S(1)}, bf16[64,3,256]{2,1,0:T(4,128)(2,1)S(1)}, u32[]{:S(2)}, u32[]{:S(2)}) collective-permute-start(bf16[64,3,256]{2,1,0:T(4,128)(2,1)S(1)} %get-tuple-element.16), channel_id=1, source_target_pairs={{0,1},{1,2},{2,3},{3,4},{4,5},{5,6},{6,7},{7,8},{8,9},{9,10},{10,1... | collective-permute-start | bytes 294920 | tf_op jit(solution)/shard_map/ppermute | solution.py:18
  91.6 0.7 copy-start.4
  92.3 15.8 %collective-permute-start.5 = (bf16[3,38,256]{2,1,0:T(8,128)(2,1)}, bf16[3,38,256]{2,1,0:T(8,128)(2,1)}, u32[]{:S(2)}, u32[]{:S(2)}) collective-permute-start(bf16[3,38,256]{2,1,0:T(8,128)(2,1)} %pad_maximum_fusion.3), channel_id=1, source_target_pairs={{0,15},{1,14},{2,13},{3,12},{4,11},{5,10},{6,9},{7,8},{8,7},{9,6},... | collective-permute-start | bytes 175112 | tf_op jit(solution)/shard_map/ppermute | solution.py:21
  94.2 13.2 %copy-start.5 = (bf16[64,3,256]{2,1,0:T(4,128)(2,1)S(1)}, bf16[64,3,256]{2,1,0:T(4,128)(2,1)}, u32[]{:S(2)}) copy-start(bf16[64,3,256]{2,1,0:T(4,128)(2,1)} %copy-done.4) | copy-start | bytes 294916
  94.2 14.8 %copy-start.1 = (f32[2048,256]{1,0:T(8,128)S(1)}, f32[2048,256]{1,0:T(8,128)}, u32[]{:S(2)}) copy-start(f32[2048,256]{1,0:T(8,128)} %get-tuple-element.12) | copy-start | bytes 6291460
  112.1 17.7 %copy-start.3 = (f32[7,7,256]{2,1,0:T(8,128)S(1)}, f32[7,7,256]{2,1,0:T(8,128)}, u32[]{:S(2)}) copy-start(f32[7,7,256]{2,1,0:T(8,128)} %kernel_grad.1) | copy-start | bytes 150532
